TPU v7x, 32 devices: a whole 2x2x4 slice. The times are simulated.
32 devices in a mesh: seq: 8 (over z, x), head: 4 (over y, core).
Axes of the slice: x: 2, y: 2, z: 4, core: 2. Of those that a mesh axis runs over, the one named last changes fastest.
Arguments:
- inputs: float32 [4096, 5120], P('seq', 'head'), may hold values from -3 to 3
- log_decay: float32 [80, 4096], P('head', 'seq'), may hold values from -1 to 0, as said below
- b_proj: float32 [4096, 128], P('seq'), may hold values from -0.5 to 0.5
- c_proj: float32 [4096, 128], P('seq'), may hold values from -0.5 to 0.5
- entry_states: float32 [8, 80, 64, 128], P('seq', 'head'), may hold values from -12 to 12
- out_grad: float32 [4096, 5120], P('seq', 'head'), may hold values from -3 to 3
Outputs:
- d_inputs: float32 [4096, 5120], P('seq', 'head')
- d_log_decay: float32 [80, 4096], P('head', 'seq')
- d_b_proj: float32 [4096, 128], P('seq')
- d_c_proj: float32 [4096, 128], P('seq')
- entry_grad: float32 [8, 80, 64, 128], P('seq', 'head')
Inputs may be any that keep to these rules, and one draw needn't show every extreme that they name: `log_decay`: negative everywhere.
All inputs are finite; a program needn't handle non-finite values.
Results may differ from a plain program's by a relative error of at most 0.0003.
Values sent between devices are 32-bit elements; how exact they have to be, the bound alone decides.
A program may use at most 192 MiB of HBM per device.

v0:
```python
import functools

import jax
import jax.numpy as jnp
from jax import lax
from jax.experimental import pallas as pl
from jax.experimental.pallas import tpu as pltpu
from jax.sharding import PartitionSpec as P

BLOCK = 256
F32 = jnp.float32
BF16 = jnp.bfloat16
NN = (((1,), (0,)), ((), ()))
NT = (((1,), (1,)), ((), ()))
TN = (((0,), (0,)), ((), ()))


def split(value):
    high = value.astype(BF16)
    return high, (value - high.astype(F32)).astype(BF16)


def dot(a, b, dims):
    return lax.dot_general(a, b, dims, preferred_element_type=F32)


def dot3(a, b, dims):
    return dot(a[0], b[0], dims) + dot(a[0], b[1], dims) + dot(a[1], b[0], dims)


def exact(a, b, dims):
    return lax.dot_general(a, b, dims, precision=lax.Precision.HIGHEST, preferred_element_type=F32)


def kernel(
    seq, group, width,
    x_ref, la_ref, b_ref, c_ref, s_ref, dy_ref,
    dx_ref, dla_ref, db_ref, dc_ref, eg_ref,
    acol, arow, score, wsum, bacc, cacc, v, st, local, gbuf, obuf, ey, z, gs, part, rsbuf, red, whole,
    send_sem, recv_sem, rs_send, rs_recv, ag_send, ag_recv,
):
    heads, tok = la_ref.shape
    nb = tok // BLOCK
    lanes = 2 * width
    pairs = heads // 2
    half = BLOCK // 2
    k = lax.axis_index("seq")
    me = lax.axis_index("head")

    barrier = pltpu.get_barrier_semaphore()
    for other in (lax.rem(k + 1, seq), lax.rem(k + seq - 1, seq)):
        pl.semaphore_signal(barrier, inc=1, device_id={"seq": other}, device_id_type=pl.DeviceIdType.MESH)
    for step in range(1, group):
        pl.semaphore_signal(
            barrier, inc=1, device_id={"head": lax.rem(me + step, group)}, device_id_type=pl.DeviceIdType.MESH
        )

    rows_i = lax.broadcasted_iota(jnp.int32, (BLOCK, BLOCK), 0)
    cols_i = lax.broadcasted_iota(jnp.int32, (BLOCK, BLOCK), 1)
    lower = jnp.where(rows_i >= cols_i, 1.0, 0.0).astype(F32)
    upper = jnp.where(rows_i <= cols_i, 1.0, 0.0).astype(F32)
    first = lax.broadcasted_iota(jnp.int32, (BLOCK, lanes), 1) < width

    for b in range(nb):
        span = pl.ds(b * BLOCK, BLOCK)
        rates = la_ref[:, b * BLOCK:(b + 1) * BLOCK]
        sums = exact(rates, upper, NN)
        for h in range(heads):
            arow[h, :, b * BLOCK:(b + 1) * BLOCK] = sums[h:h + 1]
        column = exact(lower, rates, NT)
        for h in range(heads):
            acol[h, span, :] = jnp.broadcast_to(column[:, h:h + 1], (BLOCK, lanes))
        score[b] = jnp.where(rows_i <= cols_i, dot3(split(b_ref[span, :]), split(c_ref[span, :]), NT), 0.0)
    wsum[...] = jnp.zeros_like(wsum)
    bacc[...] = jnp.zeros_like(bacc)
    cacc[...] = jnp.zeros_like(cacc)

    def lane_span(i):
        return pl.ds(pl.multiple_of(i * lanes, lanes), lanes)

    def pair_cum(i, b):
        span = pl.ds(b * BLOCK, BLOCK)
        return jnp.where(first, acol[2 * i, span, :], acol[2 * i + 1, span, :])

    def pair_end(cum):
        return cum[BLOCK - 1:BLOCK, :]

    def row_end(i, b):
        at = pl.ds((b + 1) * BLOCK - 8, 8)
        one = jnp.broadcast_to(acol[2 * i, at, :][7:], (width, lanes))
        two = jnp.broadcast_to(acol[2 * i + 1, at, :][7:], (width, lanes))
        return jnp.concatenate([one, two], axis=0)

    @pl.loop(0, pairs)
    def _(i):
        cols = lane_span(i)
        total = None
        for b in reversed(range(nb)):
            span = pl.ds(b * BLOCK, BLOCK)
            weighted = dy_ref[span, cols] * jnp.exp(pair_cum(i, b))
            value = dot3(split(weighted), split(c_ref[span, :]), TN)
            v[b, cols, :] = value
            total = value if total is None else value + jnp.exp(row_end(i, b)) * total
        local[cols, :] = total

    pl.semaphore_wait(barrier, 2 + group - 1)

    def link(i):
        cols = lane_span(i)
        return pltpu.make_async_remote_copy(
            src_ref=obuf.at[cols, :], dst_ref=gbuf.at[cols, :],
            send_sem=send_sem, recv_sem=recv_sem.at[i],
            device_id={"seq": lax.rem(k + seq - 1, seq)}, device_id_type=pl.DeviceIdType.MESH,
        )

    def chain(i):
        cols = lane_span(i)

        @pl.when(k == seq - 1)
        def _():
            gbuf[cols, :] = jnp.zeros((lanes, gbuf.shape[1]), F32)

        @pl.when(k < seq - 1)
        def _():
            link(i).wait_recv()

        @pl.when(k > 0)
        def _():
            gap = row_end(i, 0)
            for b in range(1, nb):
                gap = gap + row_end(i, b)
            obuf[cols, :] = local[cols, :] + jnp.exp(gap) * gbuf[cols, :]
            link(i).start()

    def before(i):
        cols = lane_span(i)
        state = s_ref[cols, :]
        for b in range(nb):
            span = pl.ds(b * BLOCK, BLOCK)
            st[b, cols, :] = state
            cum = pair_cum(i, b)
            grow = jnp.exp(cum)
            x = x_ref[span, cols]
            dy = dy_ref[span, cols]
            held = split(state)
            bs = split(b_ref[span, :])
            cs = split(c_ref[span, :])
            weighted = dy * grow
            outer = dot3(cs, held, NT)
            ey[span, cols] = weighted * outer
            cacc[span, :] += dot3(split(weighted), held, NN)
            tail = jnp.exp(pair_end(cum) - cum)
            state = jnp.exp(row_end(i, b)) * state + dot3(split(x * tail), bs, TN)

            dy_high, dy_low = split(dy)
            dy_both = jnp.concatenate([dy_high, dy_low], axis=1)
            xr = pltpu.roll(x, width, 1)
            dyr = pltpu.roll(dy, width, 1)
            results = []
            for which in range(2):
                h = 2 * i + which
                own = first if which == 0 else jnp.logical_not(first)
                xd = jnp.where(own, x, xr)
                xh = xd.astype(BF16).astype(F32)
                xm = jnp.where(first, xh, xd - xh).astype(BF16)
                left = jnp.concatenate([xm, xm], axis=1)
                right = jnp.concatenate(split(jnp.where(own, dy, dyr)), axis=1)
                done = []
                qsum = None
                for part_i in range(2):
                    lo = part_i * half
                    n = BLOCK - lo
                    scol = acol[h, pl.ds(b * BLOCK + lo, half), :]
                    if n > lanes:
                        scol = jnp.concatenate([scol] * (n // lanes), axis=1)
                    trow = arow[h, :, b * BLOCK + lo:(b + 1) * BLOCK]
                    decay = jnp.exp(jnp.minimum(trow - scol, 0.0))
                    both = dot(left[lo:lo + half], right[lo:], NT)
                    mix = decay * score[b, lo:lo + half, lo:]
                    wsum[b, lo:lo + half, lo:] += decay * both
                    q = jnp.sum(mix * both, axis=0, keepdims=True)
                    if lo:
                        q = jnp.concatenate([jnp.zeros((1, lo), F32), q], axis=1)
                    qsum = q if qsum is None else qsum + q
                    mh, ml = split(mix)
                    wide = dot(mh, dy_both[lo:], NN)
                    done.append(wide[:, :lanes] + wide[:, lanes:] + dot(ml, dy_high[lo:], NN))
                z[h, :, b * BLOCK:(b + 1) * BLOCK] = qsum
                results.append(jnp.concatenate(done, axis=0))
            dx_ref[span, cols] = jnp.where(first, results[0], results[1])
        st[nb, cols, :] = state

    pick = (
        lax.broadcasted_iota(jnp.int32, (8, lanes), 1) // width
        == lax.broadcasted_iota(jnp.int32, (8, lanes), 0)
    ).astype(BF16)
    pick = jnp.concatenate([pick, pick], axis=1)

    def after(i):
        cols = lane_span(i)
        grad = gbuf[cols, :]
        for b in reversed(range(nb)):
            span = pl.ds(b * BLOCK, BLOCK)
            cum = pair_cum(i, b)
            tail = jnp.exp(pair_end(cum) - cum)
            x = x_ref[span, cols]
            held = split(grad)
            dx = dx_ref[span, cols] + tail * dot3(split(b_ref[span, :]), held, NT)
            dx_ref[span, cols] = dx
            bacc[span, :] += dot3(split(x * tail), held, NN)
            change = jnp.concatenate(split(ey[span, cols] - x * dx), axis=1)
            lines = dot(pick, change, NT)
            prod = grad * st[b + 1, cols, :]
            for which in range(2):
                at = 2 * i + which
                z[at, :, b * BLOCK:(b + 1) * BLOCK] += lines[which:which + 1, :]
                gs[b, at] = jnp.sum(prod[which * width:(which + 1) * width], axis=0, keepdims=True)
            grad = jnp.exp(row_end(i, b)) * grad + v[b, cols, :]
        eg_ref[cols, :] = grad

    @pl.loop(0, pairs + seq - 1)
    def _(i):
        j = i - (seq - 1 - k)
        live = jnp.logical_and(j >= 0, j < pairs)

        @pl.when(live)
        def _():
            chain(j)

        @pl.when(i < pairs)
        def _():
            before(i)

        @pl.when(live)
        def _():
            after(j)

    states = b_ref.shape[1]
    for b in range(nb):
        span = pl.ds(b * BLOCK, BLOCK)
        table = jnp.where(rows_i <= cols_i, wsum[b], 0.0)
        part[span, :states] = bacc[span, :] + exact(table, c_ref[span, :], NN)
        part[span, states:] = cacc[span, :] + exact(table, b_ref[span, :], TN)

    share = tok // group

    def piece(owner):
        return pl.ds(pl.multiple_of(owner * share, share), share)

    def scatter(step):
        to = lax.rem(me + step, group)
        return pltpu.make_async_remote_copy(
            src_ref=part.at[piece(to), :], dst_ref=rsbuf.at[step - 1],
            send_sem=rs_send.at[step - 1], recv_sem=rs_recv.at[step - 1],
            device_id={"head": to}, device_id_type=pl.DeviceIdType.MESH,
        )

    def gather(step):
        to = lax.rem(me + step, group)
        return pltpu.make_async_remote_copy(
            src_ref=red, dst_ref=whole.at[piece(me), :],
            send_sem=ag_send.at[step - 1], recv_sem=ag_recv.at[step - 1],
            device_id={"head": to}, device_id_type=pl.DeviceIdType.MESH,
        )

    for step in range(1, group):
        scatter(step).start()
    for b in range(nb):
        s = slice(b * BLOCK, (b + 1) * BLOCK)
        lines = jnp.concatenate([z[h, :, s] for h in range(heads)], axis=0)
        inner = jnp.concatenate([gs[b, h] for h in range(heads)], axis=0)
        dla_ref[:, s] = exact(lines, lower, NN) + jnp.sum(inner, axis=1, keepdims=True)
    mine = part[piece(me), :]
    for step in range(1, group):
        scatter(step).wait_recv()
        mine = mine + rsbuf[step - 1]
    red[...] = mine
    for step in range(1, group):
        gather(step).start()
    whole[piece(me), :] = mine
    for step in range(1, group):
        gather(step).wait_recv()
    db_ref[...] = whole[:, :states]
    dc_ref[...] = whole[:, states:]
    for step in range(1, group):
        scatter(step).wait_send()
        gather(step).wait_send()

    @pl.when(k > 0)
    def _():
        @pl.loop(0, pairs)
        def _(i):
            link(i).wait_send()


def solution(mesh):
    seq, group = mesh.shape["seq"], mesh.shape["head"]

    def per_device(inputs, log_decay, b_proj, c_proj, entry_states, out_grad):
        heads, tok = log_decay.shape
        full = inputs.shape[1]
        width = full // heads
        states = b_proj.shape[1]
        nb = tok // BLOCK
        lanes = 2 * width
        vm = pl.BlockSpec(memory_space=pltpu.VMEM)
        dx, dla, db, dc, eg = pl.pallas_call(
            functools.partial(kernel, seq, group, width),
            out_shape=[
                jax.ShapeDtypeStruct((tok, full), F32),
                jax.ShapeDtypeStruct((heads, tok), F32),
                jax.ShapeDtypeStruct((tok, states), F32),
                jax.ShapeDtypeStruct((tok, states), F32),
                jax.ShapeDtypeStruct((full, states), F32),
            ],
            in_specs=[vm] * 6,
            out_specs=[vm] * 5,
            scratch_shapes=[
                pltpu.VMEM((heads, tok, lanes), F32),
                pltpu.VMEM((heads, 1, tok), F32),
                pltpu.VMEM((nb, BLOCK, BLOCK), F32),
                pltpu.VMEM((nb, BLOCK, BLOCK), F32),
                pltpu.VMEM((tok, states), F32),
                pltpu.VMEM((tok, states), F32),
                pltpu.VMEM((nb, full, states), F32),
                pltpu.VMEM((nb + 1, full, states), F32),
                pltpu.VMEM((full, states), F32),
                pltpu.VMEM((full, states), F32),
                pltpu.VMEM((full, states), F32),
                pltpu.VMEM((tok, full), F32),
                pltpu.VMEM((heads, 1, tok), F32),
                pltpu.VMEM((nb, heads, 1, states), F32),
                pltpu.VMEM((tok, 2 * states), F32),
                pltpu.VMEM((group - 1, tok // group, 2 * states), F32),
                pltpu.VMEM((tok // group, 2 * states), F32),
                pltpu.VMEM((tok, 2 * states), F32),
                pltpu.SemaphoreType.DMA,
                pltpu.SemaphoreType.DMA((heads // 2,)),
                pltpu.SemaphoreType.DMA((group - 1,)),
                pltpu.SemaphoreType.DMA((group - 1,)),
                pltpu.SemaphoreType.DMA((group - 1,)),
                pltpu.SemaphoreType.DMA((group - 1,)),
            ],
            compiler_params=pltpu.CompilerParams(
                collective_id=0, has_side_effects=True, vmem_limit_bytes=60 * 1024 * 1024
            ),
        )(inputs, log_decay, b_proj, c_proj, entry_states.reshape(full, states), out_grad)
        return dx, dla, db, dc, eg.reshape(entry_states.shape)

    in_specs = (
        P("seq", "head"),
        P("head", "seq"),
        P("seq", None),
        P("seq", None),
        P("seq", "head", None, None),
        P("seq", "head"),
    )
    out_specs = (
        P("seq", "head"),
        P("head", "seq"),
        P("seq", None),
        P("seq", None),
        P("seq", "head", None, None),
    )
    return jax.shard_map(per_device, mesh=mesh, in_specs=in_specs, out_specs=out_specs, check_vma=False)
```

profile of v0, /device:TPU:1, one launch (start us, length us, event | category | flops | bytes accessed | tf_op | source)
XLA Modules:
  0.0 73.2 jit_solution(2388730268873155233)
XLA Ops:
  0.6 66.1 %shard_map.101 = (f32[512,1280]{1,0:T(8,128)}, f32[20,512]{1,0:T(8,128)}, f32[512,128]{1,0:T(8,128)}, f32[512,128]{1,0:T(8,128)}, f32[1280,128]{1,0:T(8,128)}) custom-call(f32[512,1280]{1,0:T(8,128)} %x_ref.1, f32[20,512]{1,0:T(8,128)} %la_ref.1, f32[512,128]{1,0:T(8,128)} %b_ref.1, f32[512,128]{1,0:T(8,128)} %c_ref.1, f32[1280,128]{1,0:T(8,128)} %bitcast.2, ...), custom_call_target="tpu_custom_call" | custom-call | tf_op jit(solution)/shard_map/pallas_call | solution.py:307
  66.8 0.0 copy-start.3
  66.8 0.0 copy-start.2
  66.8 0.0 copy-start.1
  66.8 0.0 copy-start
  66.8 3.5 %copy.16 = f32[512,1280]{1,0:T(8,128)} copy(f32[512,1280]{1,0:T(8,128)} %get-tuple-element.20) | data formatting | bytes 5242880
  70.3 0.0 copy-done.3
  70.3 0.6 copy.17
  70.9 0.0 copy-done.2
  70.9 0.7 copy.18
  71.6 0.0 copy-done.1
  71.6 0.7 copy.19
  72.3 0.0 copy-done
  72.3 0.8 %copy.20 = f32[1,20,64,128]{3,2,1,0:T(8,128)} copy(f32[1,20,64,128]{3,2,1,0:T(8,128)S(1)} %bitcast.3) | data formatting | bytes 1310720
Async XLA Ops:
  66.8 3.5 %copy-start.3 = (f32[20,512]{1,0:T(8,128)S(1)}, f32[20,512]{1,0:T(8,128)}, u32[]{:S(2)}) copy-start(f32[20,512]{1,0:T(8,128)} %get-tuple-element.21) | copy-start | bytes 122884
  66.8 4.2 %copy-start.2 = (f32[512,128]{1,0:T(8,128)S(1)}, f32[512,128]{1,0:T(8,128)}, u32[]{:S(2)}) copy-start(f32[512,128]{1,0:T(8,128)} %get-tuple-element.22) | copy-start | bytes 786436
  66.8 4.8 %copy-start.1 = (f32[512,128]{1,0:T(8,128)S(1)}, f32[512,128]{1,0:T(8,128)}, u32[]{:S(2)}) copy-start(f32[512,128]{1,0:T(8,128)} %get-tuple-element.23) | copy-start | bytes 786436
  66.8 5.5 %copy-start = (f32[1280,128]{1,0:T(8,128)S(1)}, f32[1280,128]{1,0:T(8,128)}, u32[]{:S(2)}) copy-start(f32[1280,128]{1,0:T(8,128)} %get-tuple-element.14) | copy-start | bytes 1966084
where the time goes:
time: 73.3 us; the launch traced here: 73.2 us
  Pallas kernels  66.1 us (90%)
  local copies, waits for them, and re-layouts  6.37 us (9%)
    pallas_call x1, Pallas kernels, per_device(): pl.pallas_call(functools.partial(kernel, seq, group, width), out_shape=[j...  66.1 us
    unnamed x13, local copies, waits for them, and re-layouts  6.37 us

commit v1 on v0

--- a/solution.py
+++ b/solution.py
@@ -36,8 +36,9 @@
     seq, group, width,
     x_ref, la_ref, b_ref, c_ref, s_ref, dy_ref,
     dx_ref, dla_ref, db_ref, dc_ref, eg_ref,
-    acol, arow, score, wsum, bacc, cacc, v, st, local, gbuf, obuf, ey, z, gs, part, rsbuf, red, whole,
-    send_sem, recv_sem, rs_send, rs_recv, ag_send, ag_recv,
+    acol, arow, score, wsum, bacc, cacc, v, st, local, gbuf, ey, z, gs,
+    mine_tot, mate_tot, xbuf, zbuf, zout, gout, part, rsbuf, red, whole,
+    t_sem, x_send, x_recv, z_send, z_recv, g_send, g_recv, rs_send, rs_recv, ag_send, ag_recv,
 ):
     heads, tok = la_ref.shape
     nb = tok // BLOCK
@@ -48,7 +49,12 @@
     me = lax.axis_index("head")
 
     barrier = pltpu.get_barrier_semaphore()
-    for other in (lax.rem(k + 1, seq), lax.rem(k + seq - 1, seq)):
+    late = lax.rem(k, 2)
+    mate = k + 1 - 2 * late
+    level = k // 2
+    levels = seq // 2
+    own = pairs // 2
+    for other in (mate, lax.rem(k + 2, seq), lax.rem(k + seq - 2, seq)):
         pl.semaphore_signal(barrier, inc=1, device_id={"seq": other}, device_id_type=pl.DeviceIdType.MESH)
     for step in range(1, group):
         pl.semaphore_signal(
@@ -91,8 +97,38 @@
         two = jnp.broadcast_to(acol[2 * i + 1, at, :][7:], (width, lanes))
         return jnp.concatenate([one, two], axis=0)
 
+    for h in range(heads):
+        total = acol[h, BLOCK - 1:BLOCK, :]
+        for b in range(1, nb):
+            total = total + acol[h, (b + 1) * BLOCK - 1:(b + 1) * BLOCK, :]
+        mine_tot[h] = total
+
+    def remote(src, dst, send, recv, to):
+        return pltpu.make_async_remote_copy(
+            src_ref=src, dst_ref=dst, send_sem=send, recv_sem=recv,
+            device_id={"seq": to}, device_id_type=pl.DeviceIdType.MESH,
+        )
+
+    totals = remote(mine_tot, mate_tot, t_sem.at[0], t_sem.at[1], mate)
+
+    def swap(c):
+        src = local.at[lane_span(c + (1 - late) * own), :]
+        return remote(src, xbuf.at[lane_span(c), :], x_send, x_recv.at[c], mate)
+
+    def climb(c):
+        cols = lane_span(c)
+        return remote(zout.at[cols, :], zbuf.at[cols, :], z_send, z_recv.at[c], lax.rem(k + seq - 2, seq))
+
+    def hand(c):
+        dst = gbuf.at[lane_span(c + late * own), :]
+        return remote(gout.at[lane_span(c), :], dst, g_send, g_recv.at[c], mate)
+
+    pl.semaphore_wait(barrier, 3 + group - 1)
+    totals.start()
+
     @pl.loop(0, pairs)
-    def _(i):
+    def _(turn):
+        i = lax.rem(turn + (1 - late) * own, pairs)
         cols = lane_span(i)
         total = None
         for b in reversed(range(nb)):
@@ -103,34 +139,46 @@
             total = value if total is None else value + jnp.exp(row_end(i, b)) * total
         local[cols, :] = total
 
-    pl.semaphore_wait(barrier, 2 + group - 1)
-
-    def link(i):
-        cols = lane_span(i)
-        return pltpu.make_async_remote_copy(
-            src_ref=obuf.at[cols, :], dst_ref=gbuf.at[cols, :],
-            send_sem=send_sem, recv_sem=recv_sem.at[i],
-            device_id={"seq": lax.rem(k + seq - 1, seq)}, device_id_type=pl.DeviceIdType.MESH,
-        )
-
-    def chain(i):
-        cols = lane_span(i)
-
-        @pl.when(k == seq - 1)
-        def _():
-            gbuf[cols, :] = jnp.zeros((lanes, gbuf.shape[1]), F32)
-
-        @pl.when(k < seq - 1)
-        def _():
-            link(i).wait_recv()
-
-        @pl.when(k > 0)
-        def _():
-            gap = row_end(i, 0)
-            for b in range(1, nb):
-                gap = gap + row_end(i, b)
-            obuf[cols, :] = local[cols, :] + jnp.exp(gap) * gbuf[cols, :]
-            link(i).start()
+        @pl.when(turn < own)
+        def _():
+            swap(turn).start()
+
+    totals.wait()
+
+    def rows_of(ref, i):
+        one = jnp.broadcast_to(ref[2 * i], (width, lanes))
+        two = jnp.broadcast_to(ref[2 * i + 1], (width, lanes))
+        return jnp.concatenate([one, two], axis=0)
+
+    def chain(c):
+        i = c + late * own
+        cols = lane_span(c)
+        here = lane_span(i)
+
+        @pl.when(level == levels - 1)
+        def _():
+            zbuf[cols, :] = jnp.zeros((lanes, zbuf.shape[1]), F32)
+
+        swap(c).wait_recv()
+
+        @pl.when(level < levels - 1)
+        def _():
+            climb(c).wait_recv()
+
+        ours, theirs = local[here, :], xbuf[cols, :]
+        gap, other = jnp.exp(rows_of(mine_tot, i)), jnp.exp(rows_of(mate_tot, i))
+        is_late = late == 1
+        above = zbuf[cols, :]
+        middle = jnp.where(is_late, ours, theirs) + jnp.where(is_late, gap, other) * above
+
+        @pl.when(level > 0)
+        def _():
+            zout[cols, :] = jnp.where(is_late, theirs, ours) + jnp.where(is_late, other, gap) * middle
+            climb(c).start()
+
+        gout[cols, :] = jnp.where(is_late, middle, above)
+        hand(c).start()
+        gbuf[here, :] = jnp.where(is_late, above, middle)
 
     def before(i):
         cols = lane_span(i)
@@ -218,79 +266,103 @@
             grad = jnp.exp(row_end(i, b)) * grad + v[b, cols, :]
         eg_ref[cols, :] = grad
 
-    @pl.loop(0, pairs + seq - 1)
-    def _(i):
-        j = i - (seq - 1 - k)
-        live = jnp.logical_and(j >= 0, j < pairs)
-
-        @pl.when(live)
-        def _():
-            chain(j)
-
-        @pl.when(i < pairs)
-        def _():
-            before(i)
-
-        @pl.when(live)
-        def _():
-            after(j)
-
     states = b_ref.shape[1]
-    for b in range(nb):
-        span = pl.ds(b * BLOCK, BLOCK)
-        table = jnp.where(rows_i <= cols_i, wsum[b], 0.0)
-        part[span, :states] = bacc[span, :] + exact(table, c_ref[span, :], NN)
-        part[span, states:] = cacc[span, :] + exact(table, b_ref[span, :], TN)
-
     share = tok // group
 
     def piece(owner):
         return pl.ds(pl.multiple_of(owner * share, share), share)
 
-    def scatter(step):
+    def scatter(which, step):
         to = lax.rem(me + step, group)
         return pltpu.make_async_remote_copy(
-            src_ref=part.at[piece(to), :], dst_ref=rsbuf.at[step - 1],
-            send_sem=rs_send.at[step - 1], recv_sem=rs_recv.at[step - 1],
+            src_ref=part.at[which, piece(to), :], dst_ref=rsbuf.at[which, step - 1],
+            send_sem=rs_send.at[which, step - 1], recv_sem=rs_recv.at[which, step - 1],
             device_id={"head": to}, device_id_type=pl.DeviceIdType.MESH,
         )
 
-    def gather(step):
+    def gather(which, step):
         to = lax.rem(me + step, group)
         return pltpu.make_async_remote_copy(
-            src_ref=red, dst_ref=whole.at[piece(me), :],
-            send_sem=ag_send.at[step - 1], recv_sem=ag_recv.at[step - 1],
+            src_ref=red.at[which], dst_ref=whole.at[which, piece(me), :],
+            send_sem=ag_send.at[which, step - 1], recv_sem=ag_recv.at[which, step - 1],
             device_id={"head": to}, device_id_type=pl.DeviceIdType.MESH,
         )
 
+    def reduce(which):
+        mine = part[which, piece(me), :]
+        for step in range(1, group):
+            scatter(which, step).wait_recv()
+            mine = mine + rsbuf[which, step - 1]
+        red[which] = mine
+        for step in range(1, group):
+            gather(which, step).start()
+        whole[which, piece(me), :] = mine
+
+    lag = 1 + 3 * (levels - 1 - level)
+
+    @pl.loop(0, max(pairs, own + 1 + 3 * (levels - 1)))
+    def _(turn):
+        c = turn - lag
+        live = jnp.logical_and(c >= 0, c < own)
+
+        @pl.when(live)
+        def _():
+            chain(c)
+
+        @pl.when(turn < pairs)
+        def _():
+            before(lax.rem(turn + late * own, pairs))
+
+        @pl.when(turn == pairs - 1)
+        def _():
+            for b in range(nb):
+                span = pl.ds(b * BLOCK, BLOCK)
+                table = split(jnp.where(rows_i <= cols_i, wsum[b], 0.0))
+                part[1, span, :] = cacc[span, :] + dot3(table, split(b_ref[span, :]), TN)
+                bacc[span, :] += dot3(table, split(c_ref[span, :]), NN)
+            for step in range(1, group):
+                scatter(1, step).start()
+
+        @pl.when(live)
+        def _():
+            after(c + late * own)
+
+    reduce(1)
+
+    @pl.loop(0, own)
+    def _(c):
+        hand(c).wait_recv()
+        after(c + (1 - late) * own)
+
+    part[0] = bacc[...]
     for step in range(1, group):
-        scatter(step).start()
+        scatter(0, step).start()
     for b in range(nb):
         s = slice(b * BLOCK, (b + 1) * BLOCK)
         lines = jnp.concatenate([z[h, :, s] for h in range(heads)], axis=0)
         inner = jnp.concatenate([gs[b, h] for h in range(heads)], axis=0)
         dla_ref[:, s] = exact(lines, lower, NN) + jnp.sum(inner, axis=1, keepdims=True)
-    mine = part[piece(me), :]
-    for step in range(1, group):
-        scatter(step).wait_recv()
-        mine = mine + rsbuf[step - 1]
-    red[...] = mine
-    for step in range(1, group):
-        gather(step).start()
-    whole[piece(me), :] = mine
-    for step in range(1, group):
-        gather(step).wait_recv()
-    db_ref[...] = whole[:, :states]
-    dc_ref[...] = whole[:, states:]
-    for step in range(1, group):
-        scatter(step).wait_send()
-        gather(step).wait_send()
-
-    @pl.when(k > 0)
+    reduce(0)
+    for which in (1, 0):
+        for step in range(1, group):
+            gather(which, step).wait_recv()
+        out = dc_ref if which else db_ref
+        out[...] = whole[which]
+    for which in range(2):
+        for step in range(1, group):
+            scatter(which, step).wait_send()
+            gather(which, step).wait_send()
+
+    @pl.loop(0, own)
+    def _(c):
+        swap(c).wait_send()
+        hand(c).wait_send()
+
+    @pl.when(level > 0)
     def _():
-        @pl.loop(0, pairs)
-        def _(i):
-            link(i).wait_send()
+        @pl.loop(0, own)
+        def _(c):
+            climb(c).wait_send()
 
 
 def solution(mesh):
@@ -326,20 +398,30 @@
                 pltpu.VMEM((nb + 1, full, states), F32),
                 pltpu.VMEM((full, states), F32),
                 pltpu.VMEM((full, states), F32),
-                pltpu.VMEM((full, states), F32),
                 pltpu.VMEM((tok, full), F32),
                 pltpu.VMEM((heads, 1, tok), F32),
                 pltpu.VMEM((nb, heads, 1, states), F32),
-                pltpu.VMEM((tok, 2 * states), F32),
-                pltpu.VMEM((group - 1, tok // group, 2 * states), F32),
-                pltpu.VMEM((tok // group, 2 * states), F32),
-                pltpu.VMEM((tok, 2 * states), F32),
+                pltpu.VMEM((heads, 1, lanes), F32),
+                pltpu.VMEM((heads, 1, lanes), F32),
+                pltpu.VMEM((full // 2, states), F32),
+                pltpu.VMEM((full // 2, states), F32),
+                pltpu.VMEM((full // 2, states), F32),
+                pltpu.VMEM((full // 2, states), F32),
+                pltpu.VMEM((2, tok, states), F32),
+                pltpu.VMEM((2, group - 1, tok // group, states), F32),
+                pltpu.VMEM((2, tok // group, states), F32),
+                pltpu.VMEM((2, tok, states), F32),
+                pltpu.SemaphoreType.DMA((2,)),
                 pltpu.SemaphoreType.DMA,
-                pltpu.SemaphoreType.DMA((heads // 2,)),
-                pltpu.SemaphoreType.DMA((group - 1,)),
-                pltpu.SemaphoreType.DMA((group - 1,)),
-                pltpu.SemaphoreType.DMA((group - 1,)),
-                pltpu.SemaphoreType.DMA((group - 1,)),
+                pltpu.SemaphoreType.DMA((heads // 4,)),
+                pltpu.SemaphoreType.DMA,
+                pltpu.SemaphoreType.DMA((heads // 4,)),
+                pltpu.SemaphoreType.DMA,
+                pltpu.SemaphoreType.DMA((heads // 4,)),
+                pltpu.SemaphoreType.DMA((2, group - 1)),
+                pltpu.SemaphoreType.DMA((2, group - 1)),
+                pltpu.SemaphoreType.DMA((2, group - 1)),
+                pltpu.SemaphoreType.DMA((2, group - 1)),
             ],
             compiler_params=pltpu.CompilerParams(
                 collective_id=0, has_side_effects=True, vmem_limit_bytes=60 * 1024 * 1024

time: 73.3 us -> 51.1 us (0.70)
  Pallas kernels: 66.1 us -> 43.9 us
    pallas_call x1, Pallas kernels: 66.1 us -> 43.9 us  [per_device(): pl.pallas_call(functools.partial(kernel, seq, group, width), out_shape=[j...]
where the time goes in v1:
time: 51.1 us; the launch traced here: 50.9 us
  Pallas kernels  43.9 us (86%)
  local copies, waits for them, and re-layouts  6.37 us (12%)
  between operations  0.68 us (1%)
    pallas_call x1, Pallas kernels, per_device(): pl.pallas_call(functools.partial(kernel, seq, group, width), out_shape=[j...  43.9 us
    unnamed x13, local copies, waits for them, and re-layouts  6.37 us

profile of v1, /device:TPU:1, one launch (start us, length us, event | category | flops | bytes accessed | tf_op | source)
XLA Modules:
  0.0 50.9 jit_solution(7649838197485455516)
XLA Ops:
  0.6 43.9 %shard_map.101 = (f32[512,1280]{1,0:T(8,128)}, f32[20,512]{1,0:T(8,128)}, f32[512,128]{1,0:T(8,128)}, f32[512,128]{1,0:T(8,128)}, f32[1280,128]{1,0:T(8,128)}) custom-call(f32[512,1280]{1,0:T(8,128)} %x_ref.1, f32[20,512]{1,0:T(8,128)} %la_ref.1, f32[512,128]{1,0:T(8,128)} %b_ref.1, f32[512,128]{1,0:T(8,128)} %c_ref.1, f32[1280,128]{1,0:T(8,128)} %bitcast.2, ...), custom_call_target="tpu_custom_call" | custom-call | tf_op jit(solution)/shard_map/pallas_call | solution.py:379
  44.5 0.0 copy-start.3
  44.5 0.0 copy-start.2
  44.5 0.0 copy-start.1
  44.5 0.0 copy-start
  44.5 3.5 %copy.16 = f32[512,1280]{1,0:T(8,128)} copy(f32[512,1280]{1,0:T(8,128)} %get-tuple-element.20) | data formatting | bytes 5242880
  48.0 0.0 copy-done.3
  48.0 0.6 %copy.17 = f32[20,512]{1,0:T(8,128)} copy(f32[20,512]{1,0:T(8,128)S(1)} %copy-done.3) | data formatting | bytes 81920
  48.6 0.0 copy-done.2
  48.7 0.7 %copy.18 = f32[512,128]{1,0:T(8,128)} copy(f32[512,128]{1,0:T(8,128)S(1)} %copy-done.2) | data formatting | bytes 524288
  49.4 0.0 copy-done.1
  49.4 0.7 %copy.19 = f32[512,128]{1,0:T(8,128)} copy(f32[512,128]{1,0:T(8,128)S(1)} %copy-done.1) | data formatting | bytes 524288
  50.1 0.0 copy-done
  50.1 0.8 %copy.20 = f32[1,20,64,128]{3,2,1,0:T(8,128)} copy(f32[1,20,64,128]{3,2,1,0:T(8,128)S(1)} %bitcast.3) | data formatting | bytes 1310720
Async XLA Ops:
  44.5 3.5 %copy-start.3 = (f32[20,512]{1,0:T(8,128)S(1)}, f32[20,512]{1,0:T(8,128)}, u32[]{:S(2)}) copy-start(f32[20,512]{1,0:T(8,128)} %get-tuple-element.21) | copy-start | bytes 122884
  44.5 4.2 %copy-start.2 = (f32[512,128]{1,0:T(8,128)S(1)}, f32[512,128]{1,0:T(8,128)}, u32[]{:S(2)}) copy-start(f32[512,128]{1,0:T(8,128)} %get-tuple-element.22) | copy-start | bytes 786436
  44.5 4.8 %copy-start.1 = (f32[512,128]{1,0:T(8,128)S(1)}, f32[512,128]{1,0:T(8,128)}, u32[]{:S(2)}) copy-start(f32[512,128]{1,0:T(8,128)} %get-tuple-element.23) | copy-start | bytes 786436
  44.5 5.5 %copy-start = (f32[1280,128]{1,0:T(8,128)S(1)}, f32[1280,128]{1,0:T(8,128)}, u32[]{:S(2)}) copy-start(f32[1280,128]{1,0:T(8,128)} %get-tuple-element.14) | copy-start | bytes 1966084

commit v2 on v1

--- a/solution.py
+++ b/solution.py
@@ -34,8 +34,9 @@
 
 def kernel(
     seq, group, width,
-    x_ref, la_ref, b_ref, c_ref, s_ref, dy_ref,
-    dx_ref, dla_ref, db_ref, dc_ref, eg_ref,
+    x_in, la_ref, b_ref, c_ref, s_in, dy_ref,
+    dx_out, dla_ref, db_ref, dc_ref, eg_out,
+    dx_ref, eg_ref, out_sem, x_ref, s_ref, in_sem,
     acol, arow, score, wsum, bacc, cacc, v, st, local, gbuf, ey, z, gs,
     mine_tot, mate_tot, xbuf, zbuf, zout, gout, part, rsbuf, red, whole,
     t_sem, x_send, x_recv, z_send, z_recv, g_send, g_recv, rs_send, rs_recv, ag_send, ag_recv,
@@ -47,6 +48,13 @@
     half = BLOCK // 2
     k = lax.axis_index("seq")
     me = lax.axis_index("head")
+
+    loads = (
+        pltpu.make_async_copy(x_in, x_ref, in_sem.at[0]),
+        pltpu.make_async_copy(s_in, s_ref, in_sem.at[1]),
+    )
+    for load in loads:
+        load.start()
 
     barrier = pltpu.get_barrier_semaphore()
     late = lax.rem(k, 2)
@@ -76,10 +84,6 @@
         column = exact(lower, rates, NT)
         for h in range(heads):
             acol[h, span, :] = jnp.broadcast_to(column[:, h:h + 1], (BLOCK, lanes))
-        score[b] = jnp.where(rows_i <= cols_i, dot3(split(b_ref[span, :]), split(c_ref[span, :]), NT), 0.0)
-    wsum[...] = jnp.zeros_like(wsum)
-    bacc[...] = jnp.zeros_like(bacc)
-    cacc[...] = jnp.zeros_like(cacc)
 
     def lane_span(i):
         return pl.ds(pl.multiple_of(i * lanes, lanes), lanes)
@@ -143,7 +147,15 @@
         def _():
             swap(turn).start()
 
+    for b in range(nb):
+        span = pl.ds(b * BLOCK, BLOCK)
+        score[b] = jnp.where(rows_i <= cols_i, dot3(split(b_ref[span, :]), split(c_ref[span, :]), NT), 0.0)
+    wsum[...] = jnp.zeros_like(wsum)
+    bacc[...] = jnp.zeros_like(bacc)
+    cacc[...] = jnp.zeros_like(cacc)
     totals.wait()
+    for load in loads:
+        load.wait()
 
     def rows_of(ref, i):
         one = jnp.broadcast_to(ref[2 * i], (width, lanes))
@@ -244,6 +256,13 @@
     ).astype(BF16)
     pick = jnp.concatenate([pick, pick], axis=1)
 
+    def leave(i):
+        cols = lane_span(i)
+        return (
+            pltpu.make_async_copy(dx_ref.at[:, cols], dx_out.at[:, cols], out_sem),
+            pltpu.make_async_copy(eg_ref.at[cols, :], eg_out.at[cols, :], out_sem),
+        )
+
     def after(i):
         cols = lane_span(i)
         grad = gbuf[cols, :]
@@ -265,6 +284,8 @@
                 gs[b, at] = jnp.sum(prod[which * width:(which + 1) * width], axis=0, keepdims=True)
             grad = jnp.exp(row_end(i, b)) * grad + v[b, cols, :]
         eg_ref[cols, :] = grad
+        for copy in leave(i):
+            copy.start()
 
     states = b_ref.shape[1]
     share = tok // group
@@ -353,6 +374,11 @@
             scatter(which, step).wait_send()
             gather(which, step).wait_send()
 
+    @pl.loop(0, pairs)
+    def _(i):
+        for copy in leave(i):
+            copy.wait()
+
     @pl.loop(0, own)
     def _(c):
         swap(c).wait_send()
@@ -376,6 +402,7 @@
         nb = tok // BLOCK
         lanes = 2 * width
         vm = pl.BlockSpec(memory_space=pltpu.VMEM)
+        hbm = pl.BlockSpec(memory_space=pltpu.HBM)
         dx, dla, db, dc, eg = pl.pallas_call(
             functools.partial(kernel, seq, group, width),
             out_shape=[
@@ -385,9 +412,15 @@
                 jax.ShapeDtypeStruct((tok, states), F32),
                 jax.ShapeDtypeStruct((full, states), F32),
             ],
-            in_specs=[vm] * 6,
-            out_specs=[vm] * 5,
+            in_specs=[hbm, vm, vm, vm, hbm, vm],
+            out_specs=[hbm, vm, vm, vm, hbm],
             scratch_shapes=[
+                pltpu.VMEM((tok, full), F32),
+                pltpu.VMEM((full, states), F32),
+                pltpu.SemaphoreType.DMA,
+                pltpu.VMEM((tok, full), F32),
+                pltpu.VMEM((full, states), F32),
+                pltpu.SemaphoreType.DMA((2,)),
                 pltpu.VMEM((heads, tok, lanes), F32),
                 pltpu.VMEM((heads, 1, tok), F32),
                 pltpu.VMEM((nb, BLOCK, BLOCK), F32),

time: 51.1 us -> 49.5 us (0.969)
  Pallas kernels: 43.9 us -> 42.3 us
    pallas_call x1, Pallas kernels: 43.9 us -> 42.3 us  [per_device(): pl.pallas_call(functools.partial(kernel, seq, group, width), out_shape=[j...]
where the time goes in v2:
time: 49.5 us; the launch traced here: 49.3 us
  Pallas kernels  42.3 us (85%)
  local copies, waits for them, and re-layouts  6.37 us (13%)
  between operations  0.68 us (1%)
    pallas_call x1, Pallas kernels, per_device(): pl.pallas_call(functools.partial(kernel, seq, group, width), out_shape=[j...  42.3 us
    unnamed x13, local copies, waits for them, and re-layouts  6.37 us

profile of v2, /device:TPU:1, one launch (start us, length us, event | category | flops | bytes accessed | tf_op | source)
XLA Modules:
  0.0 49.3 jit_solution(5186900596649638520)
XLA Ops:
  0.6 42.3 %shard_map.101 = (f32[512,1280]{1,0:T(8,128)}, f32[20,512]{1,0:T(8,128)}, f32[512,128]{1,0:T(8,128)}, f32[512,128]{1,0:T(8,128)}, f32[1280,128]{1,0:T(8,128)}) custom-call(f32[512,1280]{1,0:T(8,128)} %x_in.1, f32[20,512]{1,0:T(8,128)} %la_ref.1, f32[512,128]{1,0:T(8,128)} %b_ref.1, f32[512,128]{1,0:T(8,128)} %c_ref.1, f32[1280,128]{1,0:T(8,128)} %bitcast.2, ...), custom_call_target="tpu_custom_call" | custom-call | tf_op jit(solution)/shard_map/pallas_call | solution.py:406
  42.9 0.0 copy-start.3
  42.9 0.0 copy-start.2
  42.9 0.0 copy-start.1
  42.9 0.0 copy-start
  42.9 3.5 %copy.16 = f32[512,1280]{1,0:T(8,128)} copy(f32[512,1280]{1,0:T(8,128)} %get-tuple-element.20) | data formatting | bytes 5242880
  46.4 0.0 copy-done.3
  46.4 0.6 %copy.17 = f32[20,512]{1,0:T(8,128)} copy(f32[20,512]{1,0:T(8,128)S(1)} %copy-done.3) | data formatting | bytes 81920
  47.1 0.0 copy-done.2
  47.1 0.7 %copy.18 = f32[512,128]{1,0:T(8,128)} copy(f32[512,128]{1,0:T(8,128)S(1)} %copy-done.2) | data formatting | bytes 524288
  47.8 0.0 copy-done.1
  47.8 0.7 %copy.19 = f32[512,128]{1,0:T(8,128)} copy(f32[512,128]{1,0:T(8,128)S(1)} %copy-done.1) | data formatting | bytes 524288
  48.5 0.0 copy-done
  48.5 0.8 %copy.20 = f32[1,20,64,128]{3,2,1,0:T(8,128)} copy(f32[1,20,64,128]{3,2,1,0:T(8,128)S(1)} %bitcast.3) | data formatting | bytes 1310720
Async XLA Ops:
  42.9 3.5 %copy-start.3 = (f32[20,512]{1,0:T(8,128)S(1)}, f32[20,512]{1,0:T(8,128)}, u32[]{:S(2)}) copy-start(f32[20,512]{1,0:T(8,128)} %get-tuple-element.21) | copy-start | bytes 122884
  42.9 4.2 %copy-start.2 = (f32[512,128]{1,0:T(8,128)S(1)}, f32[512,128]{1,0:T(8,128)}, u32[]{:S(2)}) copy-start(f32[512,128]{1,0:T(8,128)} %get-tuple-element.22) | copy-start | bytes 786436
  42.9 4.8 %copy-start.1 = (f32[512,128]{1,0:T(8,128)S(1)}, f32[512,128]{1,0:T(8,128)}, u32[]{:S(2)}) copy-start(f32[512,128]{1,0:T(8,128)} %get-tuple-element.23) | copy-start | bytes 786436
  42.9 5.5 %copy-start = (f32[1280,128]{1,0:T(8,128)S(1)}, f32[1280,128]{1,0:T(8,128)}, u32[]{:S(2)}) copy-start(f32[1280,128]{1,0:T(8,128)} %get-tuple-element.14) | copy-start | bytes 1966084
